TPU v7x, 32 devices: a whole 2x2x4 slice. The times are simulated.
32 devices in a mesh: group: 1, req: 4 (over z), head: 4 (over y, x), pool: 2 (over core).
Axes of the slice: x: 2, y: 2, z: 4, core: 2. Of those that a mesh axis runs over, the one named last changes fastest.
Arguments:
- queries: bfloat16 [192, 4096], P(('group', 'req'), 'head'), may hold values from -128 to 128
- new_entries: bfloat16 [192, 2, 4, 256], P(('group', 'req'), None, 'head'), may hold values from -6 to 6
- cache_pages: bfloat16 [4, 416, 16, 256], P('head', ('group', 'req', 'pool')), may hold values from -6 to 6
- page_table: int32 [192, 2, 1], P(('group', 'req'), 'pool'), may hold values from 0 to 51, as said below
- cached_length: int32 [192, 2], P(('group', 'req'), 'pool'), may hold values from 1 to 16, as said below
- leave_slots: int32 [32], P(('group', 'req', 'pool')), may hold values from 0 to 50, as said below
- arrive_slots: int32 [32], P(('group', 'req', 'pool')), may hold values from 0 to 51, as said below
- residual: bfloat16 [192, 2048], P(('group', 'req', 'head')), may hold values from -5 to 5
- norm_gain: float32 [2048], replicated, may hold values from 0.5 to 1.5
- output_weight: bfloat16 [4096, 2048], P(('head', 'pool')), may hold values from -0.25 to 0.25
- expert_choice: int32 [192, 8], P(('group', 'req', 'head')), may hold values from 0 to 15, all different within a row; in each aligned block of 12 rows (0 to 11, 12 to 23, ...) at most 12 rows name the same one
- route_weight: float32 [192, 8], P(('group', 'req', 'head')), may hold values from 0.2 to 1
- gate_up: bfloat16 [16, 2, 384, 2048], P(('req', 'head'), None, 'pool'), may hold values from -0.125 to 0.125
- down_weight: bfloat16 [16, 384, 2048], P(('req', 'head'), 'pool'), may hold values from -0.3125 to 0.3125
Outputs:
- decoded: bfloat16 [192, 2048], P(('group', 'req', 'head'), 'pool')
Inputs may be any that keep to these rules, and one draw needn't show every extreme that they name: `page_table`: within each block of one index of req and one pool, the 48 entries name distinct slots, none of them among that block's leave_slots. `leave_slots`: each block's 4 entries are distinct. `arrive_slots`: each block's 4 entries are distinct slots that its page table names. `cached_length`: in every block of 48 requests and each pool some request has 16. `expert_choice`: each row names 8 distinct experts; in each aligned block of 12 rows no expert is named more than 12 times, a bound that some block reaches.
All inputs are finite; a program needn't handle non-finite values.
Results may differ from a plain program's by a relative error of at most 0.023.
Values may be sent and summed in bfloat16 or wider, within the bound.
A program may use at most 64 MiB of HBM per device.

v0:
```python
import jax
import jax.numpy as jnp
from jax import lax
from jax.sharding import PartitionSpec as P


def swapped(value, axis, apart):
    mask = 2**apart
    pairs = [(source, source ^ mask) for source in range(lax.axis_size(axis))]
    return lax.ppermute(value, axis, pairs)


def combined_all(shard, axis, join):
    gathered = jax.tree.map(
        lambda a, kind: lax.all_gather(a.astype(kind), axis),
        shard,
        (jnp.bfloat16, jnp.bfloat16, jnp.bfloat16),
    )

    def take(source):
        return jax.tree.map(
            lambda a, own: lax.dynamic_index_in_dim(a, source, 0, False).astype(own.dtype),
            gathered,
            shard,
        )

    return lax.fori_loop(
        1, lax.axis_size(axis), lambda source, state: join(state, take(source)), take(0)
    )


def merge_parts(earlier, later):
    first_max, first_denominator, first_value = earlier
    second_max, second_denominator, second_value = later
    largest = jnp.maximum(first_max, second_max)
    first_scale = jnp.exp(first_max - largest)
    second_scale = jnp.exp(second_max - largest)
    denominator = first_denominator * first_scale + second_denominator * second_scale
    weighted = first_value * first_scale[..., None] + second_value * second_scale[..., None]
    return (largest, denominator, weighted)


def local(
    queries,
    new_entries,
    cache_pages,
    page_table,
    cached_length,
    leave_slots,
    arrive_slots,
    residual,
    norm_gain,
    output_weight,
    expert_choice,
    route_weight,
    gate_up,
    down_weight,
):
    batch_size = queries.shape[0]
    group_count = cache_pages.shape[0]
    head_dim = new_entries.shape[3] // 2
    group_size = queries.shape[1] // (group_count * head_dim)
    pool_index = lax.axis_index("pool")
    outgoing = cache_pages[:, leave_slots]
    arrived = swapped(outgoing, "pool", 0)
    current = cache_pages.at[:, arrive_slots].set(arrived)
    context = current[:, page_table[:, 0, :]]
    context = context.reshape(group_count, batch_size, -1, 2 * head_dim)
    context_keys = context[..., :head_dim]
    context_values = context[..., head_dim:]
    grouped_queries = queries.reshape(batch_size, group_count, group_size, head_dim)
    score_scale = head_dim ** (-0.5)
    attention_scores = (
        jnp.einsum(
            "bgqd,gbtd->bgqt", grouped_queries, context_keys, preferred_element_type=jnp.float32
        )
        * score_scale
    )
    positions = jnp.arange(context.shape[2], dtype=jnp.int32)
    valid_mask = positions[None, :] < cached_length
    attention_scores = jnp.where(valid_mask[:, None, None, :], attention_scores, -jnp.inf)
    fresh_scores = (
        jnp.einsum(
            "bgqd,bsgd->bgqs",
            grouped_queries,
            new_entries[..., :head_dim],
            preferred_element_type=jnp.float32,
        )
        * score_scale
    )
    fresh_scores = jnp.where(pool_index == 0, fresh_scores, -jnp.inf)
    largest = jnp.maximum(jnp.max(attention_scores, axis=-1), jnp.max(fresh_scores, axis=-1))
    local_weights = jnp.exp(attention_scores - largest[..., None])
    fresh_weights = jnp.exp(fresh_scores - largest[..., None])
    denominator = jnp.sum(local_weights, axis=-1) + jnp.sum(fresh_weights, axis=-1)
    weighted = jnp.einsum("bgqt,gbtd->bgqd", local_weights, context_values.astype(jnp.float32))
    weighted = weighted + jnp.einsum(
        "bgqs,bsgd->bgqd", fresh_weights, new_entries[..., head_dim:].astype(jnp.float32)
    )
    largest, denominator, weighted = combined_all(
        (largest, denominator, weighted), "pool", merge_parts
    )
    attended = (weighted / denominator[..., None]).reshape(batch_size, -1).astype(jnp.bfloat16)
    head_width = output_weight.shape[0]
    own_heads = lax.dynamic_slice_in_dim(attended, pool_index * head_width, head_width, 1)
    partial_value = jnp.dot(own_heads, output_weight, preferred_element_type=jnp.float32)
    rows_here = residual.shape[0]
    summed = lax.psum(partial_value.astype(jnp.bfloat16), ("head", "pool")).astype(jnp.float32)
    attention = lax.dynamic_slice_in_dim(summed, lax.axis_index("head") * rows_here, rows_here, 0)
    hidden = residual.astype(jnp.float32) + attention
    normed = (
        hidden * lax.rsqrt(jnp.mean(hidden * hidden, axis=-1, keepdims=True) + 1e-06) * norm_gain
    ).astype(jnp.bfloat16)
    expert_count = lax.axis_size("req") * lax.axis_size("head")
    top_count = expert_choice.shape[1]
    capacity = max(
        2, min(rows_here, (2 * rows_here * top_count + expert_count - 1) // expert_count)
    )
    flat_choice = expert_choice.reshape(-1)
    expert_hits = (
        flat_choice[:, None] == jnp.arange(expert_count, dtype=jnp.int32)[None, :]
    ).astype(jnp.int32)
    earlier = jnp.cumsum(expert_hits, axis=0) - expert_hits
    slot_index = jnp.sum(earlier * expert_hits, axis=1)
    target = flat_choice * capacity + slot_index
    placed = (
        target[:, None] == jnp.arange(expert_count * capacity, dtype=jnp.int32)[None, :]
    ).astype(jnp.float32)
    placed = placed.reshape(rows_here, top_count, expert_count * capacity)
    dispatch = jnp.sum(placed, axis=1).astype(jnp.bfloat16)
    combine_matrix = jnp.sum(placed * route_weight[:, :, None], axis=1)
    outgoing_rows = jnp.einsum("re,rd->ed", dispatch, normed, preferred_element_type=jnp.float32)
    outgoing_rows = outgoing_rows.astype(jnp.bfloat16).reshape(expert_count, capacity, -1)
    model_width = normed.shape[1]
    half_width = model_width // lax.axis_size("pool")
    projection = gate_up[0].reshape(-1, model_width)
    hidden_size = projection.shape[0] // 2
    received = lax.all_to_all(
        outgoing_rows, ("req", "head"), split_axis=0, concat_axis=0, tiled=True
    )
    sources = received.shape[0]
    item_count = received.shape[1]
    flat_rows = received.reshape(sources * item_count, model_width)
    projected = jnp.einsum("nd,fd->nf", flat_rows, projection, preferred_element_type=jnp.float32)
    activated = (jax.nn.silu(projected[:, :hidden_size]) * projected[:, hidden_size:]).astype(
        jnp.bfloat16
    )
    part_sum = jnp.dot(activated, down_weight[0], preferred_element_type=jnp.float32).reshape(
        sources, item_count, model_width
    )
    column_sum = lax.psum_scatter(
        part_sum.astype(jnp.bfloat16), "pool", scatter_dimension=2, tiled=True
    )
    returned = lax.all_to_all(column_sum, ("req", "head"), split_axis=0, concat_axis=0, tiled=True)
    gathered = returned.reshape(expert_count * capacity, half_width).astype(jnp.float32)
    expert_mix = jnp.dot(combine_matrix, gathered, precision=lax.Precision.HIGHEST)
    own_columns = lax.dynamic_slice_in_dim(hidden, pool_index * half_width, half_width, 1)
    return (own_columns + expert_mix).astype(jnp.bfloat16)


def solution(mesh):
    return jax.shard_map(
        local,
        mesh=mesh,
        in_specs=(
            P(("group", "req"), "head"),
            P(("group", "req"), None, "head", None),
            P("head", ("group", "req", "pool"), None, None),
            P(("group", "req"), "pool", None),
            P(("group", "req"), "pool"),
            P(("group", "req", "pool")),
            P(("group", "req", "pool")),
            P(("group", "req", "head"), None),
            P(),
            P(("head", "pool"), None),
            P(("group", "req", "head"), None),
            P(("group", "req", "head"), None),
            P(("req", "head"), None, "pool", None),
            P(("req", "head"), "pool", None),
        ),
        out_specs=P(("group", "req", "head"), "pool"),
        check_vma=False,
    )
```

profile of v0, /device:TPU:0, one launch (start us, length us, event | category | flops | bytes accessed | tf_op | source)
XLA Modules:
  0.0 159.7 jit_solution(2999815218880634779)
XLA Ops:
  6.5 0.0 copy-start
  6.5 0.0 copy-start.2
  6.5 0.0 copy-start.4
  6.5 0.0 all-reduce.2.cloned.1.call-start
  6.5 1.2 copy.73
  7.7 0.7 compare_select_fusion.1
  8.4 0.5 gather_fusion
  8.9 0.6 collective-permute-start
  9.5 0.7 fusion.23
  10.2 0.7 compare_select_fusion.2
  10.8 0.7 iota_compare_fusion.2
  11.5 0.8 copy.59
  12.3 0.1 eq.33
  12.4 0.1 fusion.12
  12.5 0.1 reduce_window_sum.11
  12.6 0.2 select_reduce_fusion.1
  12.8 0.1 reduce_sum.59
  12.9 0.9 copy.64
  13.8 1.0 fusion.25
  14.8 0.0 copy-done.4
  14.8 0.1 copy.61
  14.9 0.0 collective-permute-done
  14.9 0.6 scatter_fusion
  15.5 0.6 gather_fusion.1
  16.1 0.3 fusion.24
  16.4 0.1 fusion.14
  16.5 0.0 copy-done.2
  16.6 0.2 fusion.15
  16.8 0.1 copy.54
  16.9 1.8 %all-gather.3 = bf16[2,48,8]{1,2,0:T(8,128)(2,1)S(1)} all-gather(bf16[1,48,8]{1,2,0:T(8,128)(2,1)S(1)} %copy.54), channel_id=3, replica_groups=mesh['group'=1,'req'=4,'head'=4,'pool'=2] {'pool'}, dimensions={0}, use_global_device_ids=true | all-gather | bytes 2304 | tf_op jit(solution)/shard_map/all_gather | solution.py:15
  18.7 0.2 fusion.7
  18.9 0.1 copy.57
  19.0 1.8 %all-gather.4 = bf16[2,48,8]{1,2,0:T(8,128)(2,1)S(1)} all-gather(bf16[1,48,8]{1,2,0:T(8,128)(2,1)S(1)} %copy.57), channel_id=4, replica_groups=mesh['group'=1,'req'=4,'head'=4,'pool'=2] {'pool'}, dimensions={0}, use_global_device_ids=true | all-gather | bytes 2304 | tf_op jit(solution)/shard_map/all_gather | solution.py:15
  20.9 0.1 copy.55
  21.0 0.1 copy.58
  21.0 0.1 copy.56
  21.1 0.3 fusion.2
  21.4 1.9 %all-gather = bf16[96,8,128]{2,1,0:T(8,128)(2,1)S(1)} all-gather(bf16[48,8,128]{2,1,0:T(8,128)(2,1)S(1)} %fusion.2), channel_id=2, replica_groups=mesh['group'=1,'req'=4,'head'=4,'pool'=2] {'pool'}, dimensions={0}, use_global_device_ids=true | all-gather | bytes 294912 | tf_op jit(solution)/shard_map/all_gather | solution.py:15
  23.3 0.0 copy-start.1
  23.3 0.2 divide_convert_fusion
  23.6 0.0 copy-start.3
  23.6 0.0 copy-done
  23.6 1.2 convolution_convert_fusion.2
  24.8 0.0 all-reduce.2.cloned.1.call-update
  24.8 0.0 reduce-scatter.2.cloned.1.call-start
  24.8 0.1 convert_reduce_fusion
  25.0 56.1 %all-reduce.2.cloned.1.call-done = bf16[48,2048]{1,0:T(8,128)(2,1)} async-done(((bf16[48,2048]{1,0:T(8,128)(2,1)}), bf16[48,2048]{1,0:T(8,128)(2,1)}) %all-reduce.2.cloned.1.call-update) | async-done | bytes 196624 | tf_op jit(solution)/shard_map/psum | solution.py:108
  81.0 0.0 copy-done.1
  81.0 1.0 multiply_reduce_fusion
  82.1 0.0 copy-done.3
  82.1 1.3 convolution_convert_fusion.1
  83.4 1.3 reshape.273
  84.6 30.5 %all_to_all.10 = bf16[16,12,2048]{2,1,0:T(8,128)(2,1)} all-to-all(bf16[16,12,2048]{2,1,0:T(8,128)(2,1)S(1)} %reshape.273), channel_id=1, replica_groups=mesh['group'=1,'req'=4,'head'=4,'pool'=2] {'req','head'}, dimensions={0} | all-to-all | bytes 1572864 | tf_op jit(solution)/shard_map/all_to_all | solution.py:138
  115.1 1.3 reshape.274
  116.4 2.1 %fusion.26 = f32[192,384]{1,0:T(8,128)S(1)} fusion(bf16[192,2048]{1,0:T(8,128)(2,1)S(1)} %reshape.274, bf16[384,2048]{1,0:T(8,128)(2,1)} %bitcast.85), kind=kOutput, calls=%fused_computation.71 | convolution fusion | flops 301989888 | bytes 2654208 | tf_op jit(solution)/shard_map/nd,fd->nf/dot_general | solution.py:144
  118.5 0.1 fusion.6
  118.7 2.4 %convolution_convert_fusion = bf16[16,12,2048]{2,0,1:T(8,128)(2,1)} fusion(bf16[1,192,2048]{2,1,0:T(8,128)(2,1)} %param.27, bf16[16,12,192]{2,1,0:T(8,128)(2,1)S(1)} %dot_general.36), kind=kOutput, calls=%fused_computation.3 | convolution fusion | flops 151388160 | bytes 1646592 | tf_op jit(solution)/shard_map/dot_general | solution.py:148
  121.0 0.0 reduce-scatter.2.cloned.1.call-update
  121.1 6.6 %reduce-scatter.2.cloned.1.call-done = bf16[16,12,1024]{2,0,1:T(8,128)(2,1)} async-done(((bf16[16,12,2048]{2,0,1:T(8,128)(2,1)}), bf16[16,12,1024]{2,0,1:T(8,128)(2,1)}) %reduce-scatter.2.cloned.1.call-update) | async-done | bytes 393232 | tf_op jit(solution)/shard_map/reduce_scatter | solution.py:151
  127.6 2.0 %copy.63 = bf16[16,12,1024]{2,1,0:T(8,128)(2,1)} copy(bf16[16,12,1024]{2,0,1:T(8,128)(2,1)} %reduce-scatter.2.cloned.1.call-done) | data formatting | bytes 786432 | tf_op jit(solution)/shard_map/reduce_scatter | solution.py:151
  129.6 6.7 %all-to-all-start.1 = ((bf16[16,12,1024]{2,1,0:T(8,128)(2,1)}), bf16[16,12,1024]{2,1,0:T(8,128)(2,1)S(1)}, u32[]{:S(2)}, u32[]{:S(2)}) async-start(bf16[16,12,1024]{2,1,0:T(8,128)(2,1)} %copy.63), calls=%async_computation.2 | async-start | bytes 1048576 | tf_op jit(solution)/shard_map/all_to_all | solution.py:154
  136.4 15.5 %all-to-all-done.1 = bf16[16,12,1024]{2,1,0:T(8,128)(2,1)S(1)} async-done(((bf16[16,12,1024]{2,1,0:T(8,128)(2,1)}), bf16[16,12,1024]{2,1,0:T(8,128)(2,1)S(1)}, u32[]{:S(2)}, u32[]{:S(2)}) %all-to-all-start.1) | async-done | bytes 393248 | tf_op jit(solution)/shard_map/all_to_all | solution.py:154
  151.9 0.1 reshape.275
  151.9 0.9 fusion.4
  (9 shorter events, 0.1 us)
Async XLA Ops:
  6.5 17.1 %copy-start = (bf16[512,2048]{1,0:T(8,128)(2,1)S(1)}, bf16[512,2048]{1,0:T(8,128)(2,1)}, u32[]{:S(2)}) copy-start(bf16[512,2048]{1,0:T(8,128)(2,1)} %param.23) | copy-start | bytes 6291460
  6.5 10.0 %copy-start.2 = (bf16[48,2,1,256]{3,1,2,0:T(2,128)(2,1)S(1)}, bf16[48,2,1,256]{3,1,2,0:T(2,128)(2,1)}, u32[]{:S(2)}) copy-start(bf16[48,2,1,256]{3,1,2,0:T(2,128)(2,1)} %param.15) | copy-start | bytes 147460
  6.5 8.3 %copy-start.4 = (f32[12,8]{0,1:T(8,128)S(1)}, f32[12,8]{0,1:T(8,128)}, u32[]{:S(2)}) copy-start(f32[12,8]{0,1:T(8,128)} %param.25) | copy-start | bytes 1156
  6.5 74.5 %all-reduce.2.cloned.1.call-start = ((), (), s32[]{:S(2)}) async-start(), calls=%async_computation.3 | async-start | bytes 393216 | tf_op jit(solution)/shard_map/psum | solution.py:108
  8.9 6.0 %collective-permute-start = (bf16[1,4,16,256]{3,2,1,0:T(8,128)(2,1)S(1)}, bf16[1,4,16,256]{3,2,1,0:T(8,128)(2,1)S(1)}, u32[]{:S(2)}, u32[]{:S(2)}) collective-permute-start(bf16[1,4,16,256]{3,2,1,0:T(8,128)(2,1)S(1)} %bitcast.94), channel_id=1, source_target_pairs={{0,1},{1,0},{2,3},{3,2},{4,5},{5,4},{6,7},{7,6},{8,9},{9,8},{10,11... | collective-permute-start | bytes 98312 | tf_op jit(solution)/shard_map/ppermute | solution.py:10
  23.3 57.7 %copy-start.1 = (bf16[12,2048]{1,0:T(8,128)(2,1)S(1)}, bf16[12,2048]{1,0:T(8,128)(2,1)}, u32[]{:S(2)}) copy-start(bf16[12,2048]{1,0:T(8,128)(2,1)} %param.21) | copy-start | bytes 147460
  23.6 58.5 %copy-start.3 = (f32[2048]{0:T(1024)S(1)}, f32[2048]{0:T(1024)}, u32[]{:S(2)}) copy-start(f32[2048]{0:T(1024)} %param.22) | copy-start | bytes 24580
  24.8 102.8 %reduce-scatter.2.cloned.1.call-start = ((), (), s32[]{:S(2)}) async-start(), calls=%async_computation.4 | async-start | bytes 1179648 | tf_op jit(solution)/shard_map/reduce_scatter | solution.py:151
  129.6 22.2 %all-to-all-start.1 = ((bf16[16,12,1024]{2,1,0:T(8,128)(2,1)}), bf16[16,12,1024]{2,1,0:T(8,128)(2,1)S(1)}, u32[]{:S(2)}, u32[]{:S(2)}) async-start(bf16[16,12,1024]{2,1,0:T(8,128)(2,1)} %copy.63), calls=%async_computation.2 | async-start | bytes 1048576 | tf_op jit(solution)/shard_map/all_to_all | solution.py:154
Sparse Core Ops, SparseCore 0:
  24.9 56.0 all-reduce.1
  121.2 6.3 reduce-scatter.1
where the time goes:
time: 160 us
  waiting for transfers between devices  78.1 us (49%)
  blocking collectives  36.1 us (23%)
  between operations  13.6 us (8%)
  local copies, waits for them, and re-layouts  10 us (6%)
  matrix products  9.56 us (6%)
  starting transfers between devices  7.33 us (5%)
  other arithmetic  4.95 us (3%)
    psum x1, waiting for transfers between devices, local(): lax.psum(partial_value.astype(jnp.bfloat16), ('head', 'pool'))  56.1 us
    all_to_all x1, blocking collectives, local(): lax.all_to_all(outgoing_rows, ('req', 'head'), split_axis=0, concat_axis=...  30.5 us
    all_to_all x1, waiting for transfers between devices, local(): lax.all_to_all(column_sum, ('req', 'head'), split_axis=0, concat_axis=0,...  15.5 us
    all_to_all x1, starting transfers between devices, local(): lax.all_to_all(column_sum, ('req', 'head'), split_axis=0, concat_axis=0,...  6.73 us
    reduce_scatter x1, waiting for transfers between devices, local(): lax.psum_scatter(part_sum.astype(jnp.bfloat16), 'pool', scatter_dimension...  6.55 us
    all_gather x3, blocking collectives, combined_all(): lax.all_gather(a.astype(kind), axis)  5.63 us
  transfers between devices with their start and end apart: 4, of which 3 were waited for; matrix products, arithmetic and copies ran while one was open for 3% of the time, Pallas kernels for 0%

commit v1 on v0

--- a/solution.py
+++ b/solution.py
@@ -2,6 +2,11 @@
 import jax.numpy as jnp
 from jax import lax
 from jax.sharding import PartitionSpec as P
+
+
+def axis_by_axis(array, first, second):
+    partial = lax.psum(array, first)
+    return lax.psum(partial, second)
 
 
 def swapped(value, axis, apart):
@@ -105,7 +110,7 @@
     own_heads = lax.dynamic_slice_in_dim(attended, pool_index * head_width, head_width, 1)
     partial_value = jnp.dot(own_heads, output_weight, preferred_element_type=jnp.float32)
     rows_here = residual.shape[0]
-    summed = lax.psum(partial_value.astype(jnp.bfloat16), ("head", "pool")).astype(jnp.float32)
+    summed = axis_by_axis(partial_value.astype(jnp.bfloat16), "pool", "head").astype(jnp.float32)
     attention = lax.dynamic_slice_in_dim(summed, lax.axis_index("head") * rows_here, rows_here, 0)
     hidden = residual.astype(jnp.float32) + attention
     normed = (

time: 160 us -> 172 us (1.075)
  waiting for transfers between devices: 78.1 us -> 88.7 us
    psum x1 -> x2, waiting for transfers between devices: 56.1 us -> 66.5 us  [the longest x1 46.4 us: axis_by_axis(): return lax.psum(partial, second)]
  transfers between devices with their start and end apart: 4 -> 5, of which waited for: 3 -> 4; matrix products, arithmetic and copies ran while one was open for 3% -> 3% of each run, Pallas kernels for 0% -> 0%
where the time goes in v1:
time: 172 us; the launch traced here: 171 us
  waiting for transfers between devices  88.7 us (52%)
  blocking collectives  37 us (22%)
  between operations  13.4 us (8%)
  local copies, waits for them, and re-layouts  10 us (6%)
  matrix products  9.57 us (6%)
  starting transfers between devices  7.38 us (4%)
  other arithmetic  4.94 us (3%)
    psum x1, waiting for transfers between devices, axis_by_axis(): return lax.psum(partial, second)  46.4 us
    all_to_all x1, blocking collectives, local(): lax.all_to_all(outgoing_rows, ('req', 'head'), split_axis=0, concat_axis=...  31.3 us
    psum x1, waiting for transfers between devices, axis_by_axis(): partial = lax.psum(array, first)  20.1 us
    all_to_all x1, waiting for transfers between devices, local(): lax.all_to_all(column_sum, ('req', 'head'), split_axis=0, concat_axis=0,...  15.5 us
    all_to_all x1, starting transfers between devices, local(): lax.all_to_all(column_sum, ('req', 'head'), split_axis=0, concat_axis=0,...  6.74 us
    reduce_scatter x1, waiting for transfers between devices, local(): lax.psum_scatter(part_sum.astype(jnp.bfloat16), 'pool', scatter_dimension...  6.66 us
    all_gather x3, blocking collectives, combined_all(): lax.all_gather(a.astype(kind), axis)  5.63 us
  transfers between devices with their start and end apart: 5, of which 4 were waited for; matrix products, arithmetic and copies ran while one was open for 3% of the time, Pallas kernels for 0%

profile of v1, /device:TPU:0, one launch (start us, length us, event | category | flops | bytes accessed | tf_op | source)
XLA Modules:
  0.0 170.9 jit_solution(14365725323530638952)
XLA Ops:
  6.5 0.0 copy-start
  6.5 0.0 all-reduce.3.cloned.1.call-start
  6.5 1.2 copy.74
  7.7 0.7 compare_select_fusion.1
  8.4 0.5 gather_fusion
  8.9 0.6 collective-permute-start
  9.5 0.7 fusion.23
  10.2 0.7 compare_select_fusion.2
  10.8 0.7 iota_compare_fusion.2
  11.5 0.9 copy.64
  12.5 1.0 fusion.25
  13.4 0.8 copy.59
  14.2 0.1 eq.33
  14.3 0.0 collective-permute-done
  14.3 0.6 scatter_fusion
  14.9 0.6 gather_fusion.1
  15.5 0.3 fusion.24
  15.8 0.1 fusion.14
  15.9 0.0 copy-done.2
  15.9 0.2 fusion.15
  16.2 0.1 copy.54
  16.3 1.8 %all-gather.3 = bf16[2,48,8]{1,2,0:T(8,128)(2,1)S(1)} all-gather(bf16[1,48,8]{1,2,0:T(8,128)(2,1)S(1)} %copy.54), channel_id=3, replica_groups=mesh['group'=1,'req'=4,'head'=4,'pool'=2] {'pool'}, dimensions={0}, use_global_device_ids=true | all-gather | bytes 2304 | tf_op jit(solution)/shard_map/all_gather | solution.py:20
  18.1 0.2 fusion.7
  18.3 0.1 copy.57
  18.4 1.8 %all-gather.4 = bf16[2,48,8]{1,2,0:T(8,128)(2,1)S(1)} all-gather(bf16[1,48,8]{1,2,0:T(8,128)(2,1)S(1)} %copy.57), channel_id=4, replica_groups=mesh['group'=1,'req'=4,'head'=4,'pool'=2] {'pool'}, dimensions={0}, use_global_device_ids=true | all-gather | bytes 2304 | tf_op jit(solution)/shard_map/all_gather | solution.py:20
  20.3 0.1 copy.55
  20.3 0.1 copy.58
  20.4 0.1 copy.56
  20.5 0.3 fusion.2
  20.8 1.9 %all-gather = bf16[96,8,128]{2,1,0:T(8,128)(2,1)S(1)} all-gather(bf16[48,8,128]{2,1,0:T(8,128)(2,1)S(1)} %fusion.2), channel_id=2, replica_groups=mesh['group'=1,'req'=4,'head'=4,'pool'=2] {'pool'}, dimensions={0}, use_global_device_ids=true | all-gather | bytes 294912 | tf_op jit(solution)/shard_map/all_gather | solution.py:20
  22.7 0.2 divide_convert_fusion
  22.9 0.0 copy-start.4
  23.0 0.0 copy-start.1
  23.0 0.0 copy-done
  23.0 0.0 copy-start.3
  23.0 1.2 convolution_convert_fusion.2
  24.2 0.0 all-reduce.3.cloned.1.call-update
  24.2 0.0 all-reduce.5.cloned.1.call-start
  24.3 0.1 fusion.12
  24.3 0.1 reduce_window_sum.11
  24.5 0.2 select_reduce_fusion.1
  24.7 0.1 reduce_sum.59
  24.7 20.1 %all-reduce.3.cloned.1.call-done = bf16[48,2048]{1,0:T(8,128)(2,1)} async-done(((bf16[48,2048]{1,0:T(8,128)(2,1)}), bf16[48,2048]{1,0:T(8,128)(2,1)}) %all-reduce.3.cloned.1.call-update) | async-done | bytes 196624 | tf_op jit(solution)/shard_map/psum | solution.py:8
  44.8 0.0 all-reduce.5.cloned.1.call-update
  44.9 0.0 reduce-scatter.2.cloned.1.call-start
  44.9 0.0 copy-done.4
  44.9 0.1 copy.61
  45.0 0.1 convert_reduce_fusion
  45.1 46.4 %all-reduce.5.cloned.1.call-done = bf16[48,2048]{1,0:T(8,128)(2,1)} async-done(((bf16[48,2048]{1,0:T(8,128)(2,1)}), bf16[48,2048]{1,0:T(8,128)(2,1)}) %all-reduce.5.cloned.1.call-update) | async-done | bytes 196624 | tf_op jit(solution)/shard_map/psum | solution.py:9
  91.5 1.0 multiply_reduce_fusion
  92.6 1.3 convolution_convert_fusion.1
  93.9 1.3 reshape.273
  95.2 31.3 %all_to_all.10 = bf16[16,12,2048]{2,1,0:T(8,128)(2,1)} all-to-all(bf16[16,12,2048]{2,1,0:T(8,128)(2,1)S(1)} %reshape.273), channel_id=1, replica_groups=mesh['group'=1,'req'=4,'head'=4,'pool'=2] {'req','head'}, dimensions={0} | all-to-all | bytes 1572864 | tf_op jit(solution)/shard_map/all_to_all | solution.py:143
  126.5 1.3 reshape.274
  127.8 2.1 %fusion.26 = f32[192,384]{1,0:T(8,128)S(1)} fusion(bf16[192,2048]{1,0:T(8,128)(2,1)S(1)} %reshape.274, bf16[384,2048]{1,0:T(8,128)(2,1)} %bitcast.85), kind=kOutput, calls=%fused_computation.71 | convolution fusion | flops 301989888 | bytes 2654208 | tf_op jit(solution)/shard_map/nd,fd->nf/dot_general | solution.py:149
  129.9 0.1 fusion.6
  130.1 2.4 %convolution_convert_fusion = bf16[16,12,2048]{2,0,1:T(8,128)(2,1)} fusion(bf16[1,192,2048]{2,1,0:T(8,128)(2,1)} %param.27, bf16[16,12,192]{2,1,0:T(8,128)(2,1)S(1)} %dot_general.36), kind=kOutput, calls=%fused_computation.3 | convolution fusion | flops 151388160 | bytes 1646592 | tf_op jit(solution)/shard_map/dot_general | solution.py:153
  132.5 0.0 reduce-scatter.2.cloned.1.call-update
  132.5 6.7 %reduce-scatter.2.cloned.1.call-done = bf16[16,12,1024]{2,0,1:T(8,128)(2,1)} async-done(((bf16[16,12,2048]{2,0,1:T(8,128)(2,1)}), bf16[16,12,1024]{2,0,1:T(8,128)(2,1)}) %reduce-scatter.2.cloned.1.call-update) | async-done | bytes 393232 | tf_op jit(solution)/shard_map/reduce_scatter | solution.py:156
  139.1 2.0 %copy.63 = bf16[16,12,1024]{2,1,0:T(8,128)(2,1)} copy(bf16[16,12,1024]{2,0,1:T(8,128)(2,1)} %reduce-scatter.2.cloned.1.call-done) | data formatting | bytes 786432 | tf_op jit(solution)/shard_map/reduce_scatter | solution.py:156
  141.2 6.7 %all-to-all-start.1 = ((bf16[16,12,1024]{2,1,0:T(8,128)(2,1)}), bf16[16,12,1024]{2,1,0:T(8,128)(2,1)S(1)}, u32[]{:S(2)}, u32[]{:S(2)}) async-start(bf16[16,12,1024]{2,1,0:T(8,128)(2,1)} %copy.63), calls=%async_computation.2 | async-start | bytes 1048576 | tf_op jit(solution)/shard_map/all_to_all | solution.py:159
  147.9 15.5 %all-to-all-done.1 = bf16[16,12,1024]{2,1,0:T(8,128)(2,1)S(1)} async-done(((bf16[16,12,1024]{2,1,0:T(8,128)(2,1)}), bf16[16,12,1024]{2,1,0:T(8,128)(2,1)S(1)}, u32[]{:S(2)}, u32[]{:S(2)}) %all-to-all-start.1) | async-done | bytes 393248 | tf_op jit(solution)/shard_map/all_to_all | solution.py:159
  163.4 0.1 reshape.275
  163.5 0.9 fusion.4
  (12 shorter events, 0.1 us)
Async XLA Ops:
  6.5 16.5 %copy-start = (bf16[512,2048]{1,0:T(8,128)(2,1)S(1)}, bf16[512,2048]{1,0:T(8,128)(2,1)}, u32[]{:S(2)}) copy-start(bf16[512,2048]{1,0:T(8,128)(2,1)} %param.23) | copy-start | bytes 6291460
  6.5 9.4 %copy-start.2 = (bf16[48,2,1,256]{3,1,2,0:T(2,128)(2,1)S(1)}, bf16[48,2,1,256]{3,1,2,0:T(2,128)(2,1)}, u32[]{:S(2)}) copy-start(bf16[48,2,1,256]{3,1,2,0:T(2,128)(2,1)} %param.15) | copy-start | bytes 147460
  6.5 38.3 %all-reduce.3.cloned.1.call-start = ((), (), s32[]{:S(2)}) async-start(), calls=%async_computation.3 | async-start | bytes 393216 | tf_op jit(solution)/shard_map/psum | solution.py:8
  8.9 5.4 %collective-permute-start = (bf16[1,4,16,256]{3,2,1,0:T(8,128)(2,1)S(1)}, bf16[1,4,16,256]{3,2,1,0:T(8,128)(2,1)S(1)}, u32[]{:S(2)}, u32[]{:S(2)}) collective-permute-start(bf16[1,4,16,256]{3,2,1,0:T(8,128)(2,1)S(1)} %bitcast.94), channel_id=1, source_target_pairs={{0,1},{1,0},{2,3},{3,2},{4,5},{5,4},{6,7},{7,6},{8,9},{9,8},{10,11... | collective-permute-start | bytes 98312 | tf_op jit(solution)/shard_map/ppermute | solution.py:15
  22.9 22.0 %copy-start.4 = (f32[12,8]{0,1:T(8,128)S(1)}, f32[12,8]{0,1:T(8,128)}, u32[]{:S(2)}) copy-start(f32[12,8]{0,1:T(8,128)} %param.25) | copy-start | bytes 1156
  23.0 68.6 %copy-start.1 = (bf16[12,2048]{1,0:T(8,128)(2,1)S(1)}, bf16[12,2048]{1,0:T(8,128)(2,1)}, u32[]{:S(2)}) copy-start(bf16[12,2048]{1,0:T(8,128)(2,1)} %param.21) | copy-start | bytes 147460
  23.0 69.6 %copy-start.3 = (f32[2048]{0:T(1024)S(1)}, f32[2048]{0:T(1024)}, u32[]{:S(2)}) copy-start(f32[2048]{0:T(1024)} %param.22) | copy-start | bytes 24580
  24.2 67.3 %all-reduce.5.cloned.1.call-start = ((), (), s32[]{:S(2)}) async-start(), calls=%async_computation.4 | async-start | bytes 393216 | tf_op jit(solution)/shard_map/psum | solution.py:9
  44.9 94.3 %reduce-scatter.2.cloned.1.call-start = ((), (), s32[]{:S(2)}) async-start(), calls=%async_computation.5 | async-start | bytes 1179648 | tf_op jit(solution)/shard_map/reduce_scatter | solution.py:156
  141.2 22.2 %all-to-all-start.1 = ((bf16[16,12,1024]{2,1,0:T(8,128)(2,1)}), bf16[16,12,1024]{2,1,0:T(8,128)(2,1)S(1)}, u32[]{:S(2)}, u32[]{:S(2)}) async-start(bf16[16,12,1024]{2,1,0:T(8,128)(2,1)} %copy.63), calls=%async_computation.2 | async-start | bytes 1048576 | tf_op jit(solution)/shard_map/all_to_all | solution.py:159
Sparse Core Ops, SparseCore 0:
  24.3 20.4 all-reduce.2
  47.7 43.7 all-reduce.4
  132.6 6.4 reduce-scatter.1
